TPU v7x, 32 devices: a whole 2x2x4 slice. The times are simulated.
32 devices in a mesh: groups: 2 (over y), ctx: 4 (over z), section: 2 (over x), mp: 2 (over core).
Axes of the slice: x: 2, y: 2, z: 4, core: 2. Of those that a mesh axis runs over, the one named last changes fastest.
Arguments:
- spans: bfloat16 [2, 1024, 6144], P('section', ('groups', 'ctx'), 'mp'), parts along dimension 1, may hold values from -6 to 6
- norm_gain: float32 [2, 6144], P('section', 'mp'), may hold values from 0.25 to 1.75
- w_in: bfloat16 [2, 6144, 3, 4096], P('section', 'mp', None, 'ctx'), may hold values from -0.078125 to 0.078125
- filters: bfloat16 [2, 4096, 128], P('section', 'ctx'), may hold values from -0.5 to 0.5
- w_out: bfloat16 [2, 4096, 6144], P('section', 'ctx', 'mp'), may hold values from -0.09375 to 0.09375
- prompt_len: int32 [4], P(('groups', 'section')), parts along dimension 0, may hold values from 128 to 512
- needles: int32 [2, 128], P('section', 'groups'), parts along dimension 1, may hold values from 0 to 511
Outputs:
- advanced: bfloat16 [2, 1024, 6144], P('section', ('groups', 'ctx'), 'mp'), parts along dimension 1
- needle_states: bfloat16 [2, 128, 4096], P('section', 'groups', 'ctx'), parts along dimension 1
There are 2 independent parts, one for each index of `groups`. A program takes and returns all parts, laid end to end along the dimension named above; an argument that names none is the same for every part. Nothing has to cross between parts.
All inputs are finite; a program needn't handle non-finite values.
Results may differ from a plain program's by a relative error of at most 0.02.
Values may be sent and summed in bfloat16 or wider, within the bound.
No kernel may reach another device: no remote copies, remote signals or barrier semaphores. Data moves between devices by JAX's collectives and lax.ppermute only.
A program may use at most 256 MiB of HBM per device.

v0:
```python
import jax
import jax.numpy as jnp
from jax import lax
from jax.sharding import PartitionSpec as P

norm_eps = 1e-06


def shifted(value, axis, steps):
    count = lax.axis_size(axis)
    pairs = [(source, (source + steps) % count) for source in range(count)]
    return lax.ppermute(value, axis, pairs)


def band_conv(mixed, filter_taps):
    span_len, channels = mixed.shape
    tap_count = filter_taps.shape[1]
    row_idx = jnp.arange(tap_count)[:, None]
    col_idx = jnp.arange(tap_count)[None, :]
    offset = row_idx - col_idx
    table = jnp.take(filter_taps, jnp.where(offset >= 0, offset, offset + tap_count), axis=1)
    zero_band = jnp.zeros_like(table)
    near_band = jnp.where((offset >= 0)[None, :, :], table, zero_band)
    far_band = jnp.where((offset < 0)[None, :, :], table, zero_band)
    blocked = mixed.reshape(span_len // tap_count, tap_count, channels)
    previous = jnp.concatenate(
        [jnp.zeros((1, tap_count, channels), mixed.dtype), blocked[:-1]], axis=0
    )
    conv = jnp.einsum("cts,bsc->btc", near_band, blocked, preferred_element_type=jnp.float32)
    conv = conv + jnp.einsum("cts,bsc->btc", far_band, previous, preferred_element_type=jnp.float32)
    return conv.reshape(span_len, channels)


def mix_channels(proj, squares, filter_taps, live, full_width):
    scale = lax.rsqrt(squares / full_width + norm_eps)[:, None]
    query = proj[:, 0] * scale
    mixed = (proj[:, 1] * scale * (proj[:, 2] * scale) * live).astype(jnp.bfloat16)
    conv = band_conv(mixed, filter_taps)
    return (query * conv * live).astype(jnp.bfloat16)


def on_device(spans, norm_gain, w_in, filters, w_out, prompt_len, needles):
    x_local = spans[0]
    gain_local = norm_gain[0]
    w_local = w_in[0]
    half_d = x_local.shape[1]
    channels = w_local.shape[2]
    row_count = x_local.shape[0]
    span_len = row_count * lax.axis_size("ctx")
    full_width = half_d * lax.axis_size("mp")
    w_flat = w_local.reshape(half_d, 3 * channels)
    piece = lax.all_gather(x_local, "ctx", axis=0, tiled=True)
    piece_f = piece.astype(jnp.float32)
    scaled = (piece_f * gain_local[None, :]).astype(jnp.bfloat16)
    part = jnp.dot(scaled, w_flat, preferred_element_type=jnp.float32).reshape(
        piece.shape[0], 3, channels
    )
    squares = jnp.sum(piece_f * piece_f, axis=1)
    square_acc = squares
    positions = jnp.arange(span_len)
    live = (positions < prompt_len[0]).astype(jnp.float32)[:, None]
    proj, squares = (
        lax.psum(part.astype(jnp.bfloat16), "mp").astype(jnp.float32),
        lax.psum(square_acc.astype(jnp.bfloat16), "mp").astype(jnp.float32),
    )
    gated = mix_channels(proj, squares, filters[0], live, full_width)
    w_out_local = w_out[0]
    out = lax.psum_scatter(
        jnp.dot(gated, w_out_local, preferred_element_type=jnp.float32).astype(jnp.bfloat16),
        "ctx",
        scatter_dimension=0,
        tiled=True,
    ).astype(jnp.float32)
    updated = (x_local.astype(jnp.float32) + out).astype(jnp.bfloat16)
    advanced = shifted(updated, "section", 1)[None]
    one_hot = (needles[0][:, None] == positions[None, :]).astype(jnp.bfloat16)
    picked = jnp.dot(one_hot, gated, preferred_element_type=jnp.float32).astype(jnp.bfloat16)[None]
    return (advanced, picked)


def solution(mesh):
    return jax.shard_map(
        on_device,
        mesh=mesh,
        in_specs=(
            P("section", ("groups", "ctx"), "mp"),
            P("section", "mp"),
            P("section", "mp", None, "ctx"),
            P("section", "ctx", None),
            P("section", "ctx", "mp"),
            P(("groups", "section")),
            P("section", "groups"),
        ),
        out_specs=(P("section", ("groups", "ctx"), "mp"), P("section", "groups", "ctx")),
        check_vma=False,
    )
```

profile of v0, /device:TPU:0, one launch (start us, length us, event | category | flops | bytes accessed | tf_op | source)
XLA Modules:
  0.0 371.3 jit_solution(17465330520890966880)
XLA Ops:
  7.2 0.7 all-gather.3.cloned.1.call-update
  7.9 0.0 all-reduce.3.cloned.1.call-start
  8.0 24.8 %copy.16 = bf16[1,3072,3,1024]{1,3,2,0:T(8,128)(2,1)} copy(bf16[1,3072,3,1024]{3,1,2,0:T(8,128)(2,1)} %param.9) | data formatting | bytes 37748736 | tf_op args[2]
  32.7 43.0 %all-gather.3.cloned.1.call-done = bf16[1,512,3072]{2,1,0:T(8,128)(2,1)} async-done(((bf16[1,128,3072]{2,1,0:T(8,128)(2,1)}), bf16[1,512,3072]{2,1,0:T(8,128)(2,1)}) %all-gather.3.cloned.1.call-update) | async-done | bytes 3145744 | tf_op jit(solution)/shard_map/all_gather | solution.py:52
  75.7 15.9 %fusion.25 = bf16[512,3,1024]{2,0,1:T(8,128)(2,1)} fusion(bf16[1,3072,3,1024]{1,3,2,0:T(8,128)(2,1)} %copy.16, bf16[1,512,3072]{2,1,0:T(8,128)(2,1)} %all-gather.3.cloned.1.call-done, f32[3072]{0:T(1024)S(1)} %bitcast.96), kind=kOutput, calls=%fused_computation.26 | convolution fusion | flops 9669967872 | bytes 25178112 | tf_op jit(solution)/shard_map/dot_general | solution.py:55
  91.7 0.0 reduce-scatter.2.cloned.1.call-start
  92.4 0.2 copy-done.6
  92.6 0.1 copy.20
  92.8 70.0 %gather_fusion = bf16[16384,1024]{1,0:T(8,128)(2,1)} fusion(bf16[1024,128]{0,1:T(8,128)(2,1)S(1)} %bitcast.86, s32[16384]{0:T(1024)S(1)} %fusion.45), kind=kCustom, calls=%fused_computation | custom fusion | bytes 67174400 | tf_op jit(solution)/shard_map/jit(_take)/gather | solution.py:21
  162.8 46.1 %copy.21 = bf16[128,128,1024]{1,0,2:T(8,128)(2,1)} copy(bf16[128,128,1024]{2,1,0:T(8,128)(2,1)} %bitcast.87) | data formatting | bytes 67108864 | tf_op jit(solution)/shard_map/jit(_take)/gather | solution.py:21
  209.0 0.7 fusion.15
  209.7 2.6 psum.15
  212.4 4.7 %fusion.59 = (f32[512,1,1024]{2,0,1:T(8,128)}, f32[512,1,1024]{2,0,1:T(8,128)}, f32[512,1,1024]{2,0,1:T(8,128)}) fusion(bf16[512,3,1024]{2,0,1:T(8,128)(2,1)} %all-reduce.3.cloned.1.call-done), kind=kLoop, calls=%fused_computation.74 | loop fusion | bytes 12582912 | tf_op jit(solution)/shard_map/slice | solution.py:36
  217.1 3.1 copy.17
  220.2 0.7 convert_element_type.62
  220.9 0.6 slice_bitcast_fusion.1
  221.5 2.0 copy-done.1
  223.5 0.3 fusion.34
  223.8 0.7 copy.22
  224.6 3.1 copy.19
  227.7 1.8 copy.18
  229.5 22.9 %fusion = f32[1024,4,128]{2,1,0:T(4,128)} fusion(pred[128,128]{1,0:T(8,128)(4,1)S(1)} %get-tuple-element.11, bf16[128,128,1024]{1,0,2:T(8,128)(2,1)} %copy.21, pred[128,128]{1,0:T(8,128)(4,1)S(1)} %get-tuple-element.12, bf16[3,128,1024]{1,0,2:T(4,128)(2,1)S(1)} %copy.22), kind=kOutput, calls=%fused_computation.1 | convolution fusion | flops 167772160 | bytes 36470784 | tf_op jit(solution)/shard_map/cts,bsc->btc/dot_general | solution.py:30
  252.4 23.4 %multiply_convert_fusion = (bf16[4,128,1024]{1,0,2:T(4,128)(2,1)S(1)}, f32[4,128,1024]{1,0,2:T(4,128)}) fusion(f32[4,128,1024]{1,0,2:T(4,128)S(1)} %copy-done.5, f32[4,128]{1,0:T(4,128)S(1)} %fusion.52, f32[4,128]{1,0:T(4,128)S(1)} %get-tuple-element.7, f32[1024,4,128]{2,1,0:T(4,128)} %fusion, pred[128,128]{1,0:T(8,128)(4,1)S(1)} %fusion.48, ...), kind=kOutput, calls=%fused_computation.31 | convolution fusion | flops 173015040 | bytes 45125632 | tf_op jit(solution)/shard_map/cts,bsc->btc/dot_general | solution.py:29
  275.8 7.6 %fusion.18 = bf16[512,3072]{1,0:T(8,128)(2,1)} fusion(bf16[1,1024,3072]{2,1,0:T(8,128)(2,1)} %param.11, bf16[128,8,4,128]{3,2,1,0:T(4,128)(2,1)S(1)} %bitcast.97), kind=kOutput, calls=%fused_computation.22 | convolution fusion | flops 3222798336 | bytes 10485760 | tf_op jit(solution)/shard_map/dot_general | solution.py:69
  283.4 59.2 %reduce-scatter.2.cloned.1.call-done = bf16[128,3072]{1,0:T(8,128)(2,1)} async-done(((bf16[512,3072]{1,0:T(8,128)(2,1)}), bf16[128,3072]{1,0:T(8,128)(2,1)}) %reduce-scatter.2.cloned.1.call-update) | async-done | bytes 786448 | tf_op jit(solution)/shard_map/reduce_scatter | solution.py:68
  342.6 2.2 fusion.35
  344.9 1.5 collective-permute-start
  346.3 1.9 copy.23
  348.3 2.2 fusion.31
  350.5 1.0 fusion.38
  351.4 12.5 %collective-permute-done = bf16[128,3072]{1,0:T(8,128)(2,1)S(1)} collective-permute-done((bf16[128,3072]{1,0:T(8,128)(2,1)}, bf16[128,3072]{1,0:T(8,128)(2,1)S(1)}, u32[]{:S(2)}, u32[]{:S(2)}) %collective-permute-start) | collective-permute-done | bytes 786464 | tf_op jit(solution)/shard_map/ppermute | solution.py:12
  363.9 0.9 copy.32
  (26 shorter events, 0.2 us)
Async XLA Ops:
  7.2 68.6 %all-gather.3.cloned.1.call-start = ((), (), s32[]{:S(2)}) async-start(), calls=%async_computation.3 | async-start | bytes 3932160 | tf_op jit(solution)/shard_map/all_gather | solution.py:52
  7.9 67.8 %copy-start.8 = (f32[1,3072]{1,0:T(1,128)S(1)}, f32[1,3072]{1,0:T(1,128)}, u32[]{:S(2)}) copy-start(f32[1,3072]{1,0:T(1,128)} %param.8) | copy-start | bytes 36868
  7.9 204.5 %all-reduce.3.cloned.1.call-start = ((), (), s32[]{:S(2)}) async-start(), calls=%async_computation.1 | async-start | bytes 6291456 | tf_op jit(solution)/shard_map/psum | solution.py:63
  91.7 0.9 copy-start.6
  91.7 250.9 %reduce-scatter.2.cloned.1.call-start = ((), (), s32[]{:S(2)}) async-start(), calls=%async_computation.2 | async-start | bytes 3932160 | tf_op jit(solution)/shard_map/reduce_scatter | solution.py:68
  162.8 46.2 %copy-start.3 = (bf16[1,512,3072]{2,1,0:T(8,128)(2,1)S(1)}, bf16[1,512,3072]{2,1,0:T(8,128)(2,1)}, u32[]{:S(2)}) copy-start(bf16[1,512,3072]{2,1,0:T(8,128)(2,1)} %all-gather.3.cloned.1.call-done) | copy-start | bytes 9437188
  217.1 3.1 copy-start
  220.9 2.6 copy-start.1
  224.6 3.1 copy-start.2
  229.5 22.9 %copy-start.5 = (f32[4,128,1024]{1,0,2:T(4,128)S(1)}, f32[4,128,1024]{1,0,2:T(4,128)}, u32[]{:S(2)}) copy-start(f32[4,128,1024]{1,0,2:T(4,128)} %copy.17) | copy-start | bytes 6291460
  283.4 59.2 %copy-start.4 = (bf16[1,128,3072]{2,1,0:T(8,128)(2,1)S(1)}, bf16[1,128,3072]{2,1,0:T(8,128)(2,1)}, u32[]{:S(2)}) copy-start(bf16[1,128,3072]{2,1,0:T(8,128)(2,1)} %param.7) | copy-start | bytes 2359300
  344.9 19.1 %collective-permute-start = (bf16[128,3072]{1,0:T(8,128)(2,1)}, bf16[128,3072]{1,0:T(8,128)(2,1)S(1)}, u32[]{:S(2)}, u32[]{:S(2)}) collective-permute-start(bf16[128,3072]{1,0:T(8,128)(2,1)} %fusion.35), channel_id=1, source_target_pairs={{0,2},{2,0},{1,3},{3,1},{4,6},{6,4},{5,7},{7,5},{8,10},{10,8},{9,1... | collective-permute-start | bytes 2359304 | tf_op jit(solution)/shard_map/ppermute | solution.py:12
  348.3 2.2 copy-start.7
Sparse Core Ops, SparseCore 0:
  9.5 66.1 all-gather.2
  91.8 21.9 all-reduce.2
  283.6 59.0 reduce-scatter.1
where the time goes:
time: 373 us; the launch traced here: 371 us
  local copies, waits for them, and re-layouts  160 us (43%)
  waiting for transfers between devices  115 us (31%)
  matrix products  70.8 us (19%)
  between operations  14.6 us (4%)
  other arithmetic  6.21 us (2%)
    gather x2, local copies, waits for them, and re-layouts, band_conv(): jnp.take(filter_taps, jnp.where(offset >= 0, offset, offset + tap_count),...  116 us
    reduce_scatter x1, waiting for transfers between devices, on_device(): lax.psum_scatter(jnp.dot(gated, w_out_local, preferred_element_type=jnp.f...  59.2 us
    all_gather x1, waiting for transfers between devices, on_device(): piece = lax.all_gather(x_local, 'ctx', axis=0, tiled=True)  43 us
    unnamed x21, local copies, waits for them, and re-layouts  28 us
    dot_general x1, matrix products, band_conv(): jnp.einsum('cts,bsc->btc', near_band, blocked, preferred_element_type=jnp...  23.4 us
    dot_general x1, matrix products, band_conv(): jnp.einsum('cts,bsc->btc', far_band, previous, preferred_element_type=jnp...  22.9 us
    dot_general x1, matrix products, on_device(): jnp.dot(scaled, w_flat, preferred_element_type=jnp.float32)  15.9 us
    ppermute x1, waiting for transfers between devices, shifted(): return lax.ppermute(value, axis, pairs)  12.5 us
  transfers between devices with their start and end apart: 4, of which 3 were waited for; matrix products, arithmetic and copies ran while one was open for 40% of the time, Pallas kernels for 0%

commit v1 on v0

--- a/solution.py
+++ b/solution.py
@@ -49,7 +49,12 @@
     span_len = row_count * lax.axis_size("ctx")
     full_width = half_d * lax.axis_size("mp")
     w_flat = w_local.reshape(half_d, 3 * channels)
-    piece = lax.all_gather(x_local, "ctx", axis=0, tiled=True)
+    ring = [x_local]
+    for hop in range(3):
+        ring.append(lax.ppermute(ring[-1], "ctx", [(dev, (dev + 1) % 4) for dev in range(4)]))
+    piece = jnp.roll(
+        jnp.concatenate(ring[::-1], axis=0), (lax.axis_index("ctx") + 1) * ring[0].shape[0], axis=0
+    )
     piece_f = piece.astype(jnp.float32)
     scaled = (piece_f * gain_local[None, :]).astype(jnp.bfloat16)
     part = jnp.dot(scaled, w_flat, preferred_element_type=jnp.float32).reshape(

time: 373 us -> 382 us (1.024)
  local copies, waits for them, and re-layouts: 160 us -> 164 us
    all_gather x1 -> x0, waiting for transfers between devices: 43 us -> none  [on_device(): piece = lax.all_gather(x_local, 'ctx', axis=0, tiled=True)]
    ppermute x0 -> x3, waiting for transfers between devices: none -> 40.3 us  [on_device(): lax.ppermute(ring[-1], 'ctx', [(dev, (dev + 1) % 4) for dev in range(4)])]
    unnamed x21 -> x32, local copies, waits for them, and re-layouts: 28 us -> 31.4 us
  transfers between devices with their start and end apart: 4 -> 6, of which waited for: 3 -> 4; matrix products, arithmetic and copies ran while one was open for 40% -> 39% of each run, Pallas kernels for 0% -> 0%
where the time goes in v1:
time: 382 us; the launch traced here: 380 us
  local copies, waits for them, and re-layouts  164 us (43%)
  waiting for transfers between devices  115 us (30%)
  matrix products  70.8 us (19%)
  between operations  14.9 us (4%)
  other arithmetic  8.11 us (2%)
  starting transfers between devices  4.67 us (1%)
    gather x2, local copies, waits for them, and re-layouts, band_conv(): jnp.take(filter_taps, jnp.where(offset >= 0, offset, offset + tap_count),...  116 us
    reduce_scatter x1, waiting for transfers between devices, on_device(): lax.psum_scatter(jnp.dot(gated, w_out_local, preferred_element_type=jnp.f...  61.8 us
    ppermute x3, waiting for transfers between devices, on_device(): lax.ppermute(ring[-1], 'ctx', [(dev, (dev + 1) % 4) for dev in range(4)])  40.3 us
    unnamed x32, local copies, waits for them, and re-layouts  31.4 us
    dot_general x1, matrix products, band_conv(): jnp.einsum('cts,bsc->btc', near_band, blocked, preferred_element_type=jnp...  23.3 us
    dot_general x1, matrix products, band_conv(): jnp.einsum('cts,bsc->btc', far_band, previous, preferred_element_type=jnp...  22.9 us
    dot_general x1, matrix products, on_device(): jnp.dot(scaled, w_flat, preferred_element_type=jnp.float32)  15.9 us
    ppermute x1, waiting for transfers between devices, shifted(): return lax.ppermute(value, axis, pairs)  12.5 us
  transfers between devices with their start and end apart: 6, of which 4 were waited for; matrix products, arithmetic and copies ran while one was open for 39% of the time, Pallas kernels for 0%

profile of v1, /device:TPU:0, one launch (start us, length us, event | category | flops | bytes accessed | tf_op | source)
XLA Modules:
  0.0 379.7 jit_solution(12340919357047818298)
XLA Ops:
  7.2 3.1 collective-permute-start
  10.3 19.8 %collective-permute-done = bf16[128,3072]{1,0:T(8,128)(2,1)S(1)} collective-permute-done((bf16[128,3072]{1,0:T(8,128)(2,1)}, bf16[128,3072]{1,0:T(8,128)(2,1)S(1)}, u32[]{:S(2)}, u32[]{:S(2)}) %collective-permute-start) | collective-permute-done | bytes 786464 | tf_op jit(solution)/shard_map/ppermute | solution.py:54
  30.1 20.5 %collective-permute-done.1 = bf16[128,3072]{1,0:T(8,128)(2,1)S(1)} collective-permute-done((bf16[128,3072]{1,0:T(8,128)(2,1)S(1)}, bf16[128,3072]{1,0:T(8,128)(2,1)S(1)}, u32[]{:S(2)}, u32[]{:S(2)}) %collective-permute-start.1) | collective-permute-done | bytes 786464 | tf_op jit(solution)/shard_map/ppermute | solution.py:54
  50.6 24.7 %copy.16 = bf16[1,3072,3,1024]{1,3,2,0:T(8,128)(2,1)} copy(bf16[1,3072,3,1024]{3,1,2,0:T(8,128)(2,1)} %param.9) | data formatting | bytes 37748736 | tf_op args[2]
  75.4 0.1 constant_dynamic-update-slice_fusion.6
  75.8 2.7 copy-done.5
  78.5 15.9 %fusion.25 = bf16[512,3,1024]{2,0,1:T(8,128)(2,1)} fusion(bf16[1,3072,3,1024]{1,3,2,0:T(8,128)(2,1)} %copy.16, f32[3072]{0:T(1024)S(1)} %bitcast.89, bf16[1024,3072]{1,0:T(8,128)(2,1)} %copy-done.5, s32[]{:T(128)S(6)} %select_n.55), kind=kOutput, calls=%fused_computation.26 | convolution fusion | flops 9669967872 | bytes 25178116 | tf_op jit(solution)/shard_map/dot_general | solution.py:60
  95.2 0.1 copy.20
  95.4 69.9 %gather_fusion = bf16[16384,1024]{1,0:T(8,128)(2,1)} fusion(bf16[1024,128]{0,1:T(8,128)(2,1)S(1)} %bitcast.78, s32[16384]{0:T(1024)S(1)} %fusion.44), kind=kCustom, calls=%fused_computation | custom fusion | bytes 67174400 | tf_op jit(solution)/shard_map/jit(_take)/gather | solution.py:21
  165.2 46.0 %copy.21 = bf16[128,128,1024]{1,0,2:T(8,128)(2,1)} copy(bf16[128,128,1024]{2,1,0:T(8,128)(2,1)} %bitcast.79) | data formatting | bytes 67108864 | tf_op jit(solution)/shard_map/jit(_take)/gather | solution.py:21
  211.3 2.6 fusion.15
  213.9 2.6 psum.15
  216.6 4.9 %fusion.59 = (f32[512,1,1024]{2,0,1:T(8,128)}, f32[512,1,1024]{2,0,1:T(8,128)}, f32[512,1,1024]{2,0,1:T(8,128)}) fusion(bf16[512,3,1024]{2,0,1:T(8,128)(2,1)} %all-reduce.3.cloned.1.call-done), kind=kLoop, calls=%fused_computation.82 | loop fusion | bytes 12582912 | tf_op jit(solution)/shard_map/slice | solution.py:36
  221.5 2.9 copy.17
  224.4 0.7 convert_element_type.62
  225.1 2.6 copy-done.1
  227.7 0.6 slice_bitcast_fusion.1
  228.3 0.3 fusion.34
  228.6 1.4 copy.22
  230.1 3.0 copy.19
  233.1 1.8 copy.18
  234.9 22.9 %fusion = f32[1024,4,128]{2,1,0:T(4,128)} fusion(pred[128,128]{1,0:T(8,128)(4,1)S(1)} %get-tuple-element.11, bf16[128,128,1024]{1,0,2:T(8,128)(2,1)} %copy.21, pred[128,128]{1,0:T(8,128)(4,1)S(1)} %get-tuple-element.12, bf16[3,128,1024]{1,0,2:T(4,128)(2,1)S(1)} %copy-done.7), kind=kOutput, calls=%fused_computation.1 | convolution fusion | flops 167772160 | bytes 36470784 | tf_op jit(solution)/shard_map/cts,bsc->btc/dot_general | solution.py:30
  257.8 23.3 %multiply_convert_fusion = (bf16[4,128,1024]{1,0,2:T(4,128)(2,1)S(1)}, f32[4,128,1024]{1,0,2:T(4,128)}) fusion(f32[4,128,1024]{1,0,2:T(4,128)S(1)} %copy-done.6, f32[4,128]{1,0:T(4,128)S(1)} %fusion.51, f32[4,128]{1,0:T(4,128)S(1)} %get-tuple-element.7, f32[1024,4,128]{2,1,0:T(4,128)} %fusion, pred[128,128]{1,0:T(8,128)(4,1)S(1)} %fusion.47, ...), kind=kOutput, calls=%fused_computation.31 | convolution fusion | flops 173015040 | bytes 45125632 | tf_op jit(solution)/shard_map/cts,bsc->btc/dot_general | solution.py:29
  281.1 7.7 %fusion.18 = bf16[512,3072]{1,0:T(8,128)(2,1)} fusion(bf16[1,1024,3072]{2,1,0:T(8,128)(2,1)} %param.11, bf16[128,8,4,128]{3,2,1,0:T(4,128)(2,1)S(1)} %bitcast.90), kind=kOutput, calls=%fused_computation.22 | convolution fusion | flops 3222798336 | bytes 10485760 | tf_op jit(solution)/shard_map/dot_general | solution.py:74
  288.9 61.8 %reduce-scatter.2.cloned.1.call-done = bf16[128,3072]{1,0:T(8,128)(2,1)} async-done(((bf16[512,3072]{1,0:T(8,128)(2,1)}), bf16[128,3072]{1,0:T(8,128)(2,1)}) %reduce-scatter.2.cloned.1.call-update) | async-done | bytes 786448 | tf_op jit(solution)/shard_map/reduce_scatter | solution.py:73
  350.7 2.2 add_convert_fusion
  352.9 1.5 collective-permute-start.3
  354.3 1.9 copy.23
  356.3 2.2 fusion.31
  358.5 1.0 fusion.37
  359.4 12.5 %collective-permute-done.3 = bf16[128,3072]{1,0:T(8,128)(2,1)S(1)} collective-permute-done((bf16[128,3072]{1,0:T(8,128)(2,1)}, bf16[128,3072]{1,0:T(8,128)(2,1)S(1)}, u32[]{:S(2)}, u32[]{:S(2)}) %collective-permute-start.3) | collective-permute-done | bytes 786464 | tf_op jit(solution)/shard_map/ppermute | solution.py:12
  371.9 0.9 copy.39
  (41 shorter events, 0.7 us)
Async XLA Ops:
  7.2 209.4 %all-reduce.3.cloned.1.call-start = ((), (), s32[]{:S(2)}) async-start(), calls=%async_computation.1 | async-start | bytes 6291456 | tf_op jit(solution)/shard_map/psum | solution.py:68
  7.2 22.9 %collective-permute-start = (bf16[128,3072]{1,0:T(8,128)(2,1)}, bf16[128,3072]{1,0:T(8,128)(2,1)S(1)}, u32[]{:S(2)}, u32[]{:S(2)}) collective-permute-start(bf16[128,3072]{1,0:T(8,128)(2,1)} %bitcast.83), channel_id=1, source_target_pairs={{0,4},{4,8},{8,12},{12,0},{1,5},{5,9},{9,13},{13,1},{2,6},{6,10},{... | collective-permute-start | bytes 2359304 | tf_op jit(solution)/shard_map/ppermute | solution.py:54
  30.1 20.5 %collective-permute-start.1 = (bf16[128,3072]{1,0:T(8,128)(2,1)S(1)}, bf16[128,3072]{1,0:T(8,128)(2,1)S(1)}, u32[]{:S(2)}, u32[]{:S(2)}) collective-permute-start(bf16[128,3072]{1,0:T(8,128)(2,1)S(1)} %collective-permute-done), channel_id=1, source_target_pairs={{0,4},{4,8},{8,12},{12,0},{1,5},{5,9},{9,13},{13,1},{2,6},{6,10},{... | collective-permute-start | bytes 2359304 | tf_op jit(solution)/shard_map/ppermute | solution.py:54
  50.6 24.7 %collective-permute-start.2 = (bf16[128,3072]{1,0:T(8,128)(2,1)S(1)}, bf16[128,3072]{1,0:T(8,128)(2,1)S(1)}, u32[]{:S(2)}, u32[]{:S(2)}) collective-permute-start(bf16[128,3072]{1,0:T(8,128)(2,1)S(1)} %collective-permute-done.1), channel_id=1, source_target_pairs={{0,4},{4,8},{8,12},{12,0},{1,5},{5,9},{9,13},{13,1},{2,6},{6,10},{... | collective-permute-start | bytes 2359304 | tf_op jit(solution)/shard_map/ppermute | solution.py:54
  50.6 24.9 %copy-start.3 = (bf16[1,128,3072]{2,1,0:T(8,128)(2,1)S(1)}, bf16[1,128,3072]{2,1,0:T(8,128)(2,1)}, u32[]{:S(2)}) copy-start(bf16[1,128,3072]{2,1,0:T(8,128)(2,1)} %param.7) | copy-start | bytes 2359300
  75.3 3.2 copy-start.10
  75.8 2.7 copy-start.5
  78.5 16.7 %copy-start.8 = (bf16[1,1024,128]{2,1,0:T(8,128)(2,1)S(1)}, bf16[1,1024,128]{2,1,0:T(8,128)(2,1)}, u32[]{:S(2)}) copy-start(bf16[1,1024,128]{2,1,0:T(8,128)(2,1)} %param.10) | copy-start | bytes 786436
  94.5 256.2 %reduce-scatter.2.cloned.1.call-start = ((), (), s32[]{:S(2)}) async-start(), calls=%async_computation.2 | async-start | bytes 3932160 | tf_op jit(solution)/shard_map/reduce_scatter | solution.py:73
  216.6 7.8 %copy-start = (bf16[512,3,1024]{2,0,1:T(8,128)(2,1)S(1)}, bf16[512,3,1024]{2,0,1:T(8,128)(2,1)}, u32[]{:S(2)}) copy-start(bf16[512,3,1024]{2,0,1:T(8,128)(2,1)} %all-reduce.3.cloned.1.call-done) | copy-start | bytes 9437188
  225.1 2.6 copy-start.1
  228.3 4.8 %copy-start.2 = (f32[512,1,1024]{2,0,1:T(8,128)S(1)}, f32[512,1,1024]{2,0,1:T(8,128)}, u32[]{:S(2)}) copy-start(f32[512,1,1024]{2,0,1:T(8,128)} %get-tuple-element.5) | copy-start | bytes 6291460
  230.1 4.8 %copy-start.7 = (bf16[3,128,1024]{1,0,2:T(4,128)(2,1)S(1)}, bf16[3,128,1024]{1,0,2:T(4,128)(2,1)}, u32[]{:S(2)}) copy-start(bf16[3,128,1024]{1,0,2:T(4,128)(2,1)} %copy.22) | copy-start | bytes 2359300
  234.9 22.9 %copy-start.6 = (f32[4,128,1024]{1,0,2:T(4,128)S(1)}, f32[4,128,1024]{1,0,2:T(4,128)}, u32[]{:S(2)}) copy-start(f32[4,128,1024]{1,0,2:T(4,128)} %copy.17) | copy-start | bytes 6291460
  281.1 69.5 %copy-start.4 = (bf16[1,128,3072]{2,1,0:T(8,128)(2,1)S(1)}, bf16[1,128,3072]{2,1,0:T(8,128)(2,1)}, u32[]{:S(2)}) copy-start(bf16[1,128,3072]{2,1,0:T(8,128)(2,1)} %param.7) | copy-start | bytes 2359300
  288.8 69.6 %copy-start.9 = (s32[1,64]{1,0:T(1,128)S(1)}, s32[1,64]{1,0:T(1,128)}, u32[]{:S(2)}) copy-start(s32[1,64]{1,0:T(1,128)} %param.13) | copy-start | bytes 772
  352.9 19.1 %collective-permute-start.3 = (bf16[128,3072]{1,0:T(8,128)(2,1)}, bf16[128,3072]{1,0:T(8,128)(2,1)S(1)}, u32[]{:S(2)}, u32[]{:S(2)}) collective-permute-start(bf16[128,3072]{1,0:T(8,128)(2,1)} %add_convert_fusion), channel_id=1, source_target_pairs={{0,2},{2,0},{1,3},{3,1},{4,6},{6,4},{5,7},{7,5},{8,10},{10,8},{9,1... | collective-permute-start | bytes 2359304 | tf_op jit(solution)/shard_map/ppermute | solution.py:12
Sparse Core Ops, SparseCore 0:
  94.6 24.5 all-reduce.2
  289.0 61.6 reduce-scatter.1
